TPU v7x, 128 devices: a whole 4x4x4 slice. The times are simulated.
128 devices in a mesh: tok: 8 (over x, core), voc: 16 (over y, z).
Axes of the slice: x: 4, y: 4, z: 4, core: 2. Of those that a mesh axis runs over, the one named last changes fastest.
Arguments:
- tokens_in: bfloat16 [1024, 4096], P(('tok', 'voc')), may hold values from -36 to 36
- gate_raw: float32 [1024, 8], P(('tok', 'voc')), may hold values from 0.05 to 1
- expert_ids: int32 [1024, 8], P(('tok', 'voc')), may hold values from 0 to 63, all different within a row; in each aligned block of 8 rows (0 to 7, 8 to 15, ...) at most 2 rows name the same one
- w_gate: bfloat16 [4096, 49152], P(None, ('tok', 'voc')), may hold values from -0.09375 to 0.09375
- w_up: bfloat16 [4096, 49152], P(None, ('tok', 'voc')), may hold values from -0.09375 to 0.09375
- w_down: bfloat16 [49152, 4096], P(('tok', 'voc')), may hold values from -0.875 to 0.875
- final_gain: float32 [4096], replicated, may hold values from 0.1 to 1.9
- teacher_head: bfloat16 [4096, 77824], P('tok', 'voc')
- student_hidden: bfloat16 [1024, 4096], P('voc', 'tok'), may hold values from -6 to 6
- student_head: bfloat16 [4096, 77824], P('tok', 'voc')
- sampled_ids: int32 [1024], P('tok'), may hold values from 0 to 77823
- token_weight: float32 [1024], P('tok'), may hold values from 2 to 32
Outputs:
- token_loss: float32 [1024], P('tok')
- hidden_grad: bfloat16 [1024, 4096], P('voc', 'tok')
Inputs may be any that keep to these rules, and one draw needn't show every extreme that they name: `expert_ids`: each row names 8 different experts; in the 8 rows of one device no expert is named by more than 2 rows, a bound that some block reaches.
All inputs are finite; a program needn't handle non-finite values.
Results may differ from a plain program's by a relative error of at most 0.01375.
Values may be sent and summed in bfloat16 or wider, within the bound.
A program may use at most 128 MiB of HBM per device.

v0:
```python
import jax
import jax.numpy as jnp
from jax import lax
from jax.sharding import PartitionSpec as P


def route_tables(expert_ids, gate_raw, experts, capacity):
    rows_here, top_k = expert_ids.shape
    flat_ids = expert_ids.reshape(-1)
    one_hot = (flat_ids[:, None] == jnp.arange(experts, dtype=jnp.int32)[None, :]).astype(jnp.int32)
    earlier = jnp.cumsum(one_hot, axis=0, dtype=jnp.int32) - one_hot
    slot_of = jnp.sum(earlier * one_hot, axis=1, dtype=jnp.int32)
    where_to = (flat_ids * capacity + slot_of).reshape(rows_here, top_k)
    columns = jnp.arange(experts * capacity, dtype=jnp.int32)
    matched = where_to[:, :, None] == columns[None, None, :]
    shares = gate_raw / jnp.sum(gate_raw, axis=1, keepdims=True)
    combine_table = jnp.sum(jnp.where(matched, shares[:, :, None], 0.0), axis=1)
    dispatch_table = jnp.transpose(jnp.any(matched, axis=1)).astype(jnp.bfloat16)
    return (dispatch_table, combine_table)


def per_device(
    tokens_in,
    gate_raw,
    expert_ids,
    w_gate,
    w_up,
    w_down,
    final_gain,
    teacher_head,
    student_hidden,
    student_head,
    sampled_ids,
    token_weight,
):
    tok_count = lax.axis_size("tok")
    voc_count = lax.axis_size("voc")
    experts = tok_count * voc_count // 2
    rows_here, top_k = expert_ids.shape
    model_width = tokens_in.shape[1]
    capacity = max(2, 2 * rows_here * top_k // experts)
    dispatch_table, combine_table = route_tables(expert_ids, gate_raw, experts, capacity)
    dispatched = jnp.dot(dispatch_table, tokens_in, preferred_element_type=jnp.float32).astype(
        jnp.bfloat16
    )
    outgoing = jnp.repeat(dispatched.reshape(experts, capacity, model_width), 2, axis=0)
    arrived = lax.all_to_all(outgoing, ("tok", "voc"), split_axis=0, concat_axis=0, tiled=True)
    expert_rows = arrived.reshape(2 * experts * capacity, model_width)
    gate_part = jnp.dot(expert_rows, w_gate, preferred_element_type=jnp.float32)
    up_part = jnp.dot(expert_rows, w_up, preferred_element_type=jnp.float32)
    hidden_units = (jax.nn.silu(gate_part) * up_part).astype(jnp.bfloat16)
    partial_out = (
        jnp.dot(hidden_units, w_down, preferred_element_type=jnp.float32)
        .astype(jnp.bfloat16)
        .reshape(2 * experts, capacity, model_width)
    )
    returned = lax.all_to_all(partial_out, ("tok", "voc"), split_axis=0, concat_axis=0, tiled=True)
    pair_sum = jnp.sum(
        returned.astype(jnp.float32).reshape(experts, 2, capacity, model_width), axis=1
    ).reshape(experts * capacity, model_width)
    expert_mix = jnp.dot(combine_table, pair_sum, precision=lax.Precision.HIGHEST)
    residual_sum = tokens_in.astype(jnp.float32) + expert_mix
    inverse = lax.rsqrt(jnp.mean(residual_sum * residual_sum, axis=1, keepdims=True) + 1e-06)
    normed = (residual_sum * inverse * final_gain[None, :]).astype(jnp.bfloat16)
    tok_rows = lax.all_gather(normed, "voc", axis=0, tiled=True)
    teacher_cols = lax.all_to_all(tok_rows, "tok", split_axis=1, concat_axis=0, tiled=True)
    student_all = lax.all_gather(student_hidden, "voc", axis=0, tiled=True)
    vocab_local = teacher_head.shape[1]
    rows_piece = teacher_cols
    teacher_logits = lax.psum_scatter(
        jnp.dot(rows_piece, teacher_head, preferred_element_type=jnp.float32).astype(jnp.bfloat16),
        "tok",
        scatter_dimension=0,
        tiled=True,
    ).astype(jnp.float32)
    rows_piece = student_all
    student_logits = lax.psum_scatter(
        jnp.dot(rows_piece, student_head, preferred_element_type=jnp.float32),
        "tok",
        scatter_dimension=0,
        tiled=True,
    )
    differ = student_logits - teacher_logits
    vocab_start = lax.axis_index("voc") * vocab_local
    picked = sampled_ids[:, None] - vocab_start == jnp.arange(vocab_local, dtype=jnp.int32)[None, :]
    picked_s = jnp.sum(jnp.where(picked, student_logits, 0.0), axis=1)
    picked_t = jnp.sum(jnp.where(picked, teacher_logits, 0.0), axis=1)
    local_tmax = jnp.max(teacher_logits, axis=1)
    local_smax = jnp.max(student_logits, axis=1)
    teacher_max, student_max = lax.pmax((local_tmax, local_smax), "voc")
    student_exp = jnp.exp(student_logits - student_max[:, None])
    teacher_sum, student_sum, cross_sum, picked_s, picked_t = lax.psum(
        (
            jnp.sum(jnp.exp(teacher_logits - teacher_max[:, None]), axis=1),
            jnp.sum(student_exp, axis=1),
            jnp.sum(student_exp * differ, axis=1),
            picked_s,
            picked_t,
        ),
        "voc",
    )
    teacher_norm = teacher_max + jnp.log(teacher_sum)
    student_norm = student_max + jnp.log(student_sum)
    expect = cross_sum / student_sum
    token_loss = (
        expect - student_norm + teacher_norm + (picked_s - student_norm) - (picked_t - teacher_norm)
    )
    student_prob = jnp.exp(student_logits - student_norm[:, None])
    logit_grad = (
        token_weight[:, None]
        * (student_prob * (differ - expect[:, None]) + picked.astype(jnp.float32) - student_prob)
    ).astype(jnp.bfloat16)
    grad_terms = lax.dot_general(
        lax.all_gather(logit_grad, "tok", axis=0, tiled=True),
        student_head,
        (((1,), (1,)), ((), ())),
        preferred_element_type=jnp.float32,
    )
    hidden_grad = lax.psum_scatter(
        grad_terms.astype(jnp.bfloat16), "voc", scatter_dimension=0, tiled=True
    )
    return (token_loss, hidden_grad)


def solution(mesh):
    in_specs = (
        P(("tok", "voc"), None),
        P(("tok", "voc"), None),
        P(("tok", "voc"), None),
        P(None, ("tok", "voc")),
        P(None, ("tok", "voc")),
        P(("tok", "voc"), None),
        P(),
        P("tok", "voc"),
        P("voc", "tok"),
        P("tok", "voc"),
        P("tok"),
        P("tok"),
    )
    out_specs = (P("tok"), P("voc", "tok"))
    return jax.shard_map(
        per_device, mesh=mesh, in_specs=in_specs, out_specs=out_specs, check_vma=False
    )
```

profile of v0, /device:TPU:0, one launch (start us, length us, event | category | flops | bytes accessed | tf_op | source)
XLA Modules:
  0.0 612.6 jit_solution(13637765129616562563)
XLA Ops:
  7.2 0.0 copy-start
  7.2 0.9 eq.20
  8.1 0.1 fusion.12
  8.2 0.1 reduce_window_sum.11
  8.3 0.2 select_reduce_fusion.2
  8.5 0.1 reduce_sum.93
  8.5 0.7 multiply_add_fusion
  9.2 0.1 fusion.11
  9.3 2.3 convolution_convert_fusion.2
  11.6 2.5 reshape.54
  14.2 3.7 broadcast_in_dim.21
  17.9 40.9 %all_to_all.29 = bf16[128,2,4096]{2,1,0:T(2,128)(2,1)} all-to-all(bf16[128,2,4096]{2,1,0:T(2,128)(2,1)S(1)} %bitcast.26), channel_id=1, replica_groups=mesh['tok'=8,'voc'=16] {'tok','voc'}, dimensions={0} | all-to-all | bytes 4194304 | tf_op jit(solution)/shard_map/all_to_all | solution.py:47
  58.8 4.1 reshape.56
  62.9 3.8 fusion.15
  66.7 0.0 copy-done
  66.7 6.3 %convolution_convert_fusion.1 = bf16[256,4096]{1,0:T(8,128)(2,1)} fusion(bf16[384,4096]{1,0:T(8,128)(2,1)S(1)} %copy-done, bf16[256,4096]{1,0:T(8,128)(2,1)} %reshape.56, bf16[4096,384]{1,0:T(8,128)(2,1)} %param.16, f32[256,384]{1,0:T(8,128)S(1)} %fusion.15), kind=kOutput, calls=%fused_computation.1 | convolution fusion | flops 1612251136 | bytes 10878976 | tf_op jit(solution)/shard_map/dot_general | solution.py:53
  72.9 4.4 reshape.57
  77.3 4.8 all-to-all-start.1
  82.1 0.2 all-gather.6.cloned.1.call-start
  82.4 0.0 copy-done.4
  82.4 0.1 reduce_sum.94
  82.5 0.1 broadcast_divide_fusion
  82.6 0.1 select_reduce_fusion.1
  82.7 29.2 %all-to-all-done.1 = bf16[128,2,4096]{2,1,0:T(2,128)(2,1)S(1)} async-done(((bf16[128,2,4096]{2,1,0:T(2,128)(2,1)}), bf16[128,2,4096]{2,1,0:T(2,128)(2,1)S(1)}, u32[]{:S(2)}, u32[]{:S(2)}) %all-to-all-start.1) | async-done | bytes 2097184 | tf_op jit(solution)/shard_map/all_to_all | solution.py:57
  111.9 4.1 convert_reduce_fusion
  116.0 2.7 reshape.60
  118.8 0.0 copy-done.3
  118.8 1.2 multiply_reduce_fusion.1
  120.0 0.0 copy-done.5
  120.0 0.7 multiply_convert_fusion.1
  120.7 0.0 all-gather.6.cloned.1.call-update
  120.7 38.7 %all-gather.6.cloned.1.call-done = bf16[128,4096]{1,0:T(8,128)(2,1)} async-done(((bf16[8,4096]{1,0:T(8,128)(2,1)}), bf16[128,4096]{1,0:T(8,128)(2,1)}) %all-gather.6.cloned.1.call-update) | async-done | bytes 1048592 | tf_op jit(solution)/shard_map/all_gather | solution.py:65
  159.5 2.3 copy.18
  161.8 4.3 all-to-all-start.2
  166.1 0.0 all-gather.4.cloned.1.call-start
  166.1 0.7 all-gather.4.cloned.1.call-update
  166.8 0.0 reduce-scatter.6.cloned.1.call-start
  166.9 15.1 %all-to-all-done.2 = bf16[128,8,512]{2,0,1:T(8,128)(2,1)S(1)} async-done(((bf16[128,8,512]{2,0,1:T(8,128)(2,1)}), bf16[128,8,512]{2,0,1:T(8,128)(2,1)S(1)}, u32[]{:S(2)}, u32[]{:S(2)}) %all-to-all-start.2) | async-done | bytes 1048608 | tf_op jit(solution)/shard_map/all_to_all | solution.py:66
  182.0 10.2 %convolution_convert_fusion = bf16[1024,4864]{1,0:T(8,128)(2,1)} fusion(bf16[1024,512]{1,0:T(8,128)(2,1)S(1)} %bitcast.27, bf16[512,4864]{1,0:T(8,128)(2,1)} %param.19), kind=kOutput, calls=%fused_computation | convolution fusion | flops 5105254400 | bytes 15990784 | tf_op jit(solution)/shard_map/dot_general | solution.py:71
  192.2 0.0 reduce-scatter.6.cloned.1.call-update
  192.2 0.0 reduce-scatter.4.cloned.1.call-start
  192.2 19.2 %all-gather.4.cloned.1.call-done = bf16[1024,512]{1,0:T(8,128)(2,1)} async-done(((bf16[64,512]{1,0:T(8,128)(2,1)}), bf16[1024,512]{1,0:T(8,128)(2,1)}) %all-gather.4.cloned.1.call-update) | async-done | bytes 1048592 | tf_op jit(solution)/shard_map/all_gather | solution.py:67
  211.5 12.6 %fusion.14 = f32[1024,4864]{1,0:T(8,128)} fusion(bf16[1024,512]{1,0:T(8,128)(2,1)} %all-gather.4.cloned.1.call-done, bf16[512,4864]{1,0:T(8,128)(2,1)} %param.21), kind=kOutput, calls=%fused_computation.42 | convolution fusion | flops 5100273664 | bytes 25952256 | tf_op jit(solution)/shard_map/dot_general | solution.py:78
  224.0 0.0 reduce-scatter.4.cloned.1.call-update
  224.1 0.0 all-gather.8.cloned.1.call-start
  224.1 0.6 copy-done.7
  224.7 48.3 %reduce-scatter.6.cloned.1.call-done = bf16[128,4864]{1,0:T(8,128)(2,1)} async-done(((bf16[1024,4864]{1,0:T(8,128)(2,1)}), bf16[128,4864]{1,0:T(8,128)(2,1)}) %reduce-scatter.6.cloned.1.call-update) | async-done | bytes 1245200 | tf_op jit(solution)/shard_map/reduce_scatter | solution.py:70
  273.0 1.5 reduce_max.24
  274.6 107.0 %reduce-scatter.4.cloned.1.call-done = f32[128,4864]{1,0:T(8,128)} async-done(((f32[1024,4864]{1,0:T(8,128)}), f32[128,4864]{1,0:T(8,128)}) %reduce-scatter.4.cloned.1.call-update) | async-done | bytes 2490384 | tf_op jit(solution)/shard_map/reduce_scatter | solution.py:77
  381.6 2.0 reduce_max.23
  383.7 41.3 %all-reduce.1 = (f32[128]{0:T(128)S(1)}, f32[128]{0:T(128)S(1)}) all-reduce(f32[128]{0:T(128)S(1)} %reduce_max.23, bf16[128]{0:T(256)(128)(2,1)S(1)} %reduce_max.24), channel_id=1, replica_groups=mesh['tok'=8,'voc'=16] {'voc'}, use_global_device_ids=true, to_apply=%region_2.3 | all-reduce | flops 256 | bytes 1792 | tf_op jit(solution)/shard_map/pmax | solution.py:90
  425.0 0.0 copy-done.2
  425.0 3.6 multiply_reduce_fusion
  428.5 35.5 %all-reduce = (f32[128]{0:T(128)S(1)}, f32[128]{0:T(128)S(1)}, f32[128]{0:T(128)S(1)}, f32[128]{0:T(128)S(1)}, f32[128]{0:T(128)S(1)}) all-reduce(f32[128]{0:T(128)S(1)} %get-tuple-element.5, f32[128]{0:T(128)S(1)} %get-tuple-element.4, f32[128]{0:T(128)S(1)} %get-tuple-element.3, ...), channel_id=1, replica_groups=mesh['tok'=8,'voc'=16] {'voc'}, use_global_device_ids=true, to_apply=%region_22.23 | all-reduce | flops 640 | bytes 5120 | tf_op jit(solution)/shard_map/psum | solution.py:92
  464.0 0.5 subtract_subtract_fusion
  464.5 0.0 copy-done.6
  464.5 3.5 multiply_convert_fusion
  468.1 0.0 all-gather.8.cloned.1.call-update
  468.1 0.0 reduce-scatter.8.cloned.1.call-start
  468.1 51.9 %all-gather.8.cloned.1.call-done = bf16[1024,4864]{1,0:T(8,128)(2,1)} async-done(((bf16[128,4864]{1,0:T(8,128)(2,1)}), bf16[1024,4864]{1,0:T(8,128)(2,1)}) %all-gather.8.cloned.1.call-update) | async-done | bytes 9961488 | tf_op jit(solution)/shard_map/all_gather | solution.py:114
  520.0 11.1 %convolution_convert_fusion.3 = bf16[1024,512]{1,0:T(8,128)(2,1)} fusion(bf16[1024,4864]{1,0:T(8,128)(2,1)} %all-gather.8.cloned.1.call-done, bf16[512,4864]{1,0:T(8,128)(2,1)} %param.21), kind=kOutput, calls=%fused_computation.17 | convolution fusion | flops 5100797952 | bytes 15990784 | tf_op jit(solution)/shard_map/dot_general | solution.py:113
  531.1 0.0 reduce-scatter.8.cloned.1.call-update
  531.2 74.6 %reduce-scatter.8.cloned.1.call-done = bf16[64,512]{1,0:T(8,128)(2,1)} async-done(((bf16[1024,512]{1,0:T(8,128)(2,1)}), bf16[64,512]{1,0:T(8,128)(2,1)}) %reduce-scatter.8.cloned.1.call-update) | async-done | bytes 65552 | tf_op jit(solution)/shard_map/reduce_scatter | solution.py:119
  605.8 0.0 copy-done.1
  (9 shorter events, 0.0 us)
Async XLA Ops:
  7.2 59.5 %copy-start = (bf16[384,4096]{1,0:T(8,128)(2,1)S(1)}, bf16[384,4096]{1,0:T(8,128)(2,1)}, u32[]{:S(2)}) copy-start(bf16[384,4096]{1,0:T(8,128)(2,1)} %param.17) | copy-start | bytes 9437188
  77.3 5.0 copy-start.4
  77.3 34.6 %all-to-all-start.1 = ((bf16[128,2,4096]{2,1,0:T(2,128)(2,1)}), bf16[128,2,4096]{2,1,0:T(2,128)(2,1)S(1)}, u32[]{:S(2)}, u32[]{:S(2)}) async-start(bf16[128,2,4096]{2,1,0:T(2,128)(2,1)} %reshape.57), calls=%async_computation.2 | async-start | bytes 4194304 | tf_op jit(solution)/shard_map/all_to_all | solution.py:57
  82.1 77.4 %all-gather.6.cloned.1.call-start = ((), (), s32[]{:S(2)}) async-start(), calls=%async_computation.8 | async-start | bytes 1114112 | tf_op jit(solution)/shard_map/all_gather | solution.py:65
  116.0 2.7 copy-start.3
  116.0 4.0 copy-start.5
  161.8 20.2 %all-to-all-start.2 = ((bf16[128,8,512]{2,0,1:T(8,128)(2,1)}), bf16[128,8,512]{2,0,1:T(8,128)(2,1)S(1)}, u32[]{:S(2)}, u32[]{:S(2)}) async-start(bf16[128,8,512]{2,0,1:T(8,128)(2,1)} %bitcast.25), calls=%async_computation.3 | async-start | bytes 2097152 | tf_op jit(solution)/shard_map/all_to_all | solution.py:66
  166.1 45.4 %all-gather.4.cloned.1.call-start = ((), (), s32[]{:S(2)}) async-start(), calls=%async_computation.6 | async-start | bytes 1114112 | tf_op jit(solution)/shard_map/all_gather | solution.py:67
  166.8 106.2 %reduce-scatter.6.cloned.1.call-start = ((), (), s32[]{:S(2)}) async-start(), calls=%async_computation.9 | async-start | bytes 11206656 | tf_op jit(solution)/shard_map/reduce_scatter | solution.py:70
  192.2 189.4 %reduce-scatter.4.cloned.1.call-start = ((), (), s32[]{:S(2)}) async-start(), calls=%async_computation.7 | async-start | bytes 22413312 | tf_op jit(solution)/shard_map/reduce_scatter | solution.py:77
  224.0 0.7 copy-start.7
  224.1 296.0 %all-gather.8.cloned.1.call-start = ((), (), s32[]{:S(2)}) async-start(), calls=%async_computation.10 | async-start | bytes 11206656 | tf_op jit(solution)/shard_map/all_gather | solution.py:114
  381.6 43.4 %copy-start.2 = (f32[128,4864]{1,0:T(8,128)S(1)}, f32[128,4864]{1,0:T(8,128)}, u32[]{:S(2)}) copy-start(f32[128,4864]{1,0:T(8,128)} %reduce-scatter.4.cloned.1.call-done) | copy-start | bytes 7471108
  383.7 80.9 %copy-start.6 = (f32[128]{0:T(128)S(1)}, f32[128]{0:T(128)}, u32[]{:S(2)}) copy-start(f32[128]{0:T(128)} %param.23) | copy-start | bytes 1540
  468.1 137.7 %reduce-scatter.8.cloned.1.call-start = ((), (), s32[]{:S(2)}) async-start(), calls=%async_computation.11 | async-start | bytes 1114112 | tf_op jit(solution)/shard_map/reduce_scatter | solution.py:119
  520.0 85.7 %copy-start.1 = (bf16[384,4096]{1,0:T(8,128)(2,1)S(1)}, bf16[384,4096]{1,0:T(8,128)(2,1)}, u32[]{:S(2)}) copy-start(bf16[384,4096]{1,0:T(8,128)(2,1)} %param.17) | copy-start | bytes 9437188
Sparse Core Ops, SparseCore 0:
  120.9 38.5 all-gather.5
  169.0 42.4 all-gather.3
  213.9 59.1 reduce-scatter.5
  275.3 106.2 reduce-scatter.3
  468.2 51.7 all-gather.7
  531.3 74.4 reduce-scatter.7
where the time goes:
time: 613 us
  waiting for transfers between devices  385 us (63%)
  blocking collectives  118 us (19%)
  matrix products  47.4 us (8%)
  local copies, waits for them, and re-layouts  21.4 us (3%)
  other arithmetic  17.5 us (3%)
  between operations  14.2 us (2%)
  starting transfers between devices  9.46 us (2%)
    reduce_scatter x1, waiting for transfers between devices, per_device(): lax.psum_scatter(jnp.dot(rows_piece, student_head, preferred_element_type...  107 us
    reduce_scatter x1, waiting for transfers between devices, per_device(): lax.psum_scatter(grad_terms.astype(jnp.bfloat16), 'voc', scatter_dimensio...  74.6 us
    all_gather x1, waiting for transfers between devices, per_device(): lax.all_gather(logit_grad, 'tok', axis=0, tiled=True)  51.9 us
    reduce_scatter x1, waiting for transfers between devices, per_device(): lax.psum_scatter(jnp.dot(rows_piece, teacher_head, preferred_element_type...  48.3 us
    pmax x1, blocking collectives, per_device(): teacher_max, student_max = lax.pmax((local_tmax, local_smax), 'voc')  41.3 us
    all_to_all x1, blocking collectives, per_device(): lax.all_to_all(outgoing, ('tok', 'voc'), split_axis=0, concat_axis=0, til...  40.9 us
    all_gather x1, waiting for transfers between devices, per_device(): tok_rows = lax.all_gather(normed, 'voc', axis=0, tiled=True)  38.7 us
    psum x1, blocking collectives, per_device(): lax.psum((jnp.sum(jnp.exp(teacher_logits - teacher_max[:, None]), axis=1)...  35.5 us
  transfers between devices with their start and end apart: 8, of which 8 were waited for; matrix products, arithmetic and copies ran while one was open for 4% of the time, Pallas kernels for 0%

commit v1 on v0

--- a/solution.py
+++ b/solution.py
@@ -2,6 +2,11 @@
 import jax.numpy as jnp
 from jax import lax
 from jax.sharding import PartitionSpec as P
+from jax.lax import all_to_all, axis_size
+
+part_cells = lambda mine: jnp.concatenate(
+    all_to_all(jnp.stack([mine for _ in range(axis_size("voc"))], 0), "voc", 0, 0), axis=0
+)
 
 
 def route_tables(expert_ids, gate_raw, experts, capacity):
@@ -62,7 +67,7 @@
     residual_sum = tokens_in.astype(jnp.float32) + expert_mix
     inverse = lax.rsqrt(jnp.mean(residual_sum * residual_sum, axis=1, keepdims=True) + 1e-06)
     normed = (residual_sum * inverse * final_gain[None, :]).astype(jnp.bfloat16)
-    tok_rows = lax.all_gather(normed, "voc", axis=0, tiled=True)
+    tok_rows = part_cells(normed)
     teacher_cols = lax.all_to_all(tok_rows, "tok", split_axis=1, concat_axis=0, tiled=True)
     student_all = lax.all_gather(student_hidden, "voc", axis=0, tiled=True)
     vocab_local = teacher_head.shape[1]

time: 613 us -> 569 us (0.928)
  waiting for transfers between devices: 385 us -> 322 us
  blocking collectives: 118 us -> 138 us
    all_gather x1 -> x0, waiting for transfers between devices: 38.7 us -> none  [per_device(): tok_rows = lax.all_gather(normed, 'voc', axis=0, tiled=True)]
    reduce_scatter x1, waiting for transfers between devices: 48.3 us -> 25.1 us  [per_device(): lax.psum_scatter(jnp.dot(rows_piece, teacher_head, preferred_element_type...]
    all_to_all x0 -> x1, blocking collectives: none -> 19.9 us  [all_to_all(jnp.stack([mine for _ in range(axis_size('voc'))], 0), 'voc',...]
  transfers between devices with their start and end apart: 8 -> 7, of which waited for: 8 -> 7; matrix products, arithmetic and copies ran while one was open for 4% -> 4% of each run, Pallas kernels for 0% -> 0%
where the time goes in v1:
time: 569 us
  waiting for transfers between devices  322 us (57%)
  blocking collectives  138 us (24%)
  matrix products  47.3 us (8%)
  local copies, waits for them, and re-layouts  20.9 us (4%)
  other arithmetic  16.9 us (3%)
  between operations  15.8 us (3%)
  starting transfers between devices  8.73 us (2%)
    reduce_scatter x1, waiting for transfers between devices, per_device(): lax.psum_scatter(jnp.dot(rows_piece, student_head, preferred_element_type...  107 us
    reduce_scatter x1, waiting for transfers between devices, per_device(): lax.psum_scatter(grad_terms.astype(jnp.bfloat16), 'voc', scatter_dimensio...  74.6 us
    all_gather x1, waiting for transfers between devices, per_device(): lax.all_gather(logit_grad, 'tok', axis=0, tiled=True)  51.8 us
    pmax x1, blocking collectives, per_device(): teacher_max, student_max = lax.pmax((local_tmax, local_smax), 'voc')  41.3 us
    all_to_all x1, blocking collectives, per_device(): lax.all_to_all(outgoing, ('tok', 'voc'), split_axis=0, concat_axis=0, til...  40.9 us
    psum x1, blocking collectives, per_device(): lax.psum((jnp.sum(jnp.exp(teacher_logits - teacher_max[:, None]), axis=1)...  35.5 us
    all_to_all x1, waiting for transfers between devices, per_device(): lax.all_to_all(partial_out, ('tok', 'voc'), split_axis=0, concat_axis=0,...  29.3 us
    reduce_scatter x1, waiting for transfers between devices, per_device(): lax.psum_scatter(jnp.dot(rows_piece, teacher_head, preferred_element_type...  25.1 us
  transfers between devices with their start and end apart: 7, of which 7 were waited for; matrix products, arithmetic and copies ran while one was open for 4% of the time, Pallas kernels for 0%

profile of v1, /device:TPU:0, one launch (start us, length us, event | category | flops | bytes accessed | tf_op | source)
XLA Modules:
  0.0 568.7 jit_solution(10436294012160777815)
XLA Ops:
  8.0 0.0 copy-start
  8.0 0.9 eq.20
  8.9 0.1 fusion.12
  9.0 0.1 reduce_window_sum.11
  9.1 0.2 select_reduce_fusion.2
  9.3 0.1 reduce_sum.93
  9.4 0.7 multiply_add_fusion
  10.1 0.1 fusion.11
  10.2 2.3 convolution_convert_fusion.2
  12.5 2.5 reshape.58
  15.0 3.7 broadcast_in_dim.21
  18.7 40.9 %all_to_all.34 = bf16[128,2,4096]{2,1,0:T(2,128)(2,1)} all-to-all(bf16[128,2,4096]{2,1,0:T(2,128)(2,1)S(1)} %bitcast.25), channel_id=1, replica_groups=mesh['tok'=8,'voc'=16] {'tok','voc'}, dimensions={0} | all-to-all | bytes 4194304 | tf_op jit(solution)/shard_map/all_to_all | solution.py:52
  59.6 4.1 reshape.60
  63.7 3.8 fusion.15
  67.5 0.0 copy-done
  67.5 6.3 %convolution_convert_fusion.1 = bf16[256,4096]{1,0:T(8,128)(2,1)} fusion(bf16[384,4096]{1,0:T(8,128)(2,1)S(1)} %copy-done, bf16[256,4096]{1,0:T(8,128)(2,1)} %reshape.60, bf16[4096,384]{1,0:T(8,128)(2,1)} %param.16, f32[256,384]{1,0:T(8,128)S(1)} %fusion.15), kind=kOutput, calls=%fused_computation.1 | convolution fusion | flops 1612251136 | bytes 10878976 | tf_op jit(solution)/shard_map/dot_general | solution.py:58
  73.8 4.4 reshape.61
  78.2 5.0 all-to-all-start.1
  83.1 0.0 copy-done.4
  83.2 0.1 reduce_sum.94
  83.3 0.1 broadcast_divide_fusion
  83.3 0.1 select_reduce_fusion.1
  83.4 29.3 %all-to-all-done.1 = bf16[128,2,4096]{2,1,0:T(2,128)(2,1)S(1)} async-done(((bf16[128,2,4096]{2,1,0:T(2,128)(2,1)}), bf16[128,2,4096]{2,1,0:T(2,128)(2,1)S(1)}, u32[]{:S(2)}, u32[]{:S(2)}) %all-to-all-start.1) | async-done | bytes 2097184 | tf_op jit(solution)/shard_map/all_to_all | solution.py:62
  112.7 4.1 convert_reduce_fusion
  116.9 2.7 reshape.64
  119.6 0.0 copy-done.3
  119.6 1.2 multiply_reduce_fusion.1
  120.8 0.0 copy-done.5
  120.8 0.1 multiply_convert_fusion.1
  120.9 0.1 stack.2
  121.0 19.9 %all_to_all.35 = bf16[16,8,4096]{2,1,0:T(8,128)(2,1)S(1)} all-to-all(bf16[16,8,4096]{2,1,0:T(8,128)(2,1)S(1)} %stack.2), channel_id=1, replica_groups=mesh['tok'=8,'voc'=16] {'voc'}, dimensions={0} | all-to-all | bytes 2097152 | tf_op jit(solution)/shard_map/all_to_all | solution.py:8
  140.9 0.4 copy.17
  141.3 1.3 copy.16
  142.6 3.6 all-to-all-start.3
  146.2 0.0 all-gather.3.cloned.1.call-start
  146.2 0.7 all-gather.3.cloned.1.call-update
  146.9 0.0 reduce-scatter.6.cloned.1.call-start
  147.0 15.1 %all-to-all-done.3 = bf16[128,8,512]{2,0,1:T(8,128)(2,1)S(1)} async-done(((bf16[128,8,512]{2,0,1:T(8,128)(2,1)}), bf16[128,8,512]{2,0,1:T(8,128)(2,1)S(1)}, u32[]{:S(2)}, u32[]{:S(2)}) %all-to-all-start.3) | async-done | bytes 1048608 | tf_op jit(solution)/shard_map/all_to_all | solution.py:71
  162.1 10.2 %convolution_convert_fusion = bf16[1024,4864]{1,0:T(8,128)(2,1)} fusion(bf16[1024,512]{1,0:T(8,128)(2,1)S(1)} %bitcast.28, bf16[512,4864]{1,0:T(8,128)(2,1)} %param.19), kind=kOutput, calls=%fused_computation | convolution fusion | flops 5105254400 | bytes 15990784 | tf_op jit(solution)/shard_map/dot_general | solution.py:76
  172.2 0.0 reduce-scatter.6.cloned.1.call-update
  172.3 0.0 reduce-scatter.4.cloned.1.call-start
  172.3 18.0 %all-gather.3.cloned.1.call-done = bf16[1024,512]{1,0:T(8,128)(2,1)} async-done(((bf16[64,512]{1,0:T(8,128)(2,1)}), bf16[1024,512]{1,0:T(8,128)(2,1)}) %all-gather.3.cloned.1.call-update) | async-done | bytes 1048592 | tf_op jit(solution)/shard_map/all_gather | solution.py:72
  190.3 12.5 %fusion.14 = f32[1024,4864]{1,0:T(8,128)} fusion(bf16[1024,512]{1,0:T(8,128)(2,1)} %all-gather.3.cloned.1.call-done, bf16[512,4864]{1,0:T(8,128)(2,1)} %param.21), kind=kOutput, calls=%fused_computation.41 | convolution fusion | flops 5100273664 | bytes 25952256 | tf_op jit(solution)/shard_map/dot_general | solution.py:83
  202.8 0.0 reduce-scatter.4.cloned.1.call-update
  202.8 0.0 all-gather.5.cloned.1.call-start
  202.9 0.6 copy-done.7
  203.5 25.1 %reduce-scatter.6.cloned.1.call-done = bf16[128,4864]{1,0:T(8,128)(2,1)} async-done(((bf16[1024,4864]{1,0:T(8,128)(2,1)}), bf16[128,4864]{1,0:T(8,128)(2,1)}) %reduce-scatter.6.cloned.1.call-update) | async-done | bytes 1245200 | tf_op jit(solution)/shard_map/reduce_scatter | solution.py:75
  228.5 1.5 reduce_max.24
  230.1 107.0 %reduce-scatter.4.cloned.1.call-done = f32[128,4864]{1,0:T(8,128)} async-done(((f32[1024,4864]{1,0:T(8,128)}), f32[128,4864]{1,0:T(8,128)}) %reduce-scatter.4.cloned.1.call-update) | async-done | bytes 2490384 | tf_op jit(solution)/shard_map/reduce_scatter | solution.py:82
  337.0 2.0 reduce_max.23
  339.1 41.3 %all-reduce.1 = (f32[128]{0:T(128)S(1)}, f32[128]{0:T(128)S(1)}) all-reduce(f32[128]{0:T(128)S(1)} %reduce_max.23, bf16[128]{0:T(256)(128)(2,1)S(1)} %reduce_max.24), channel_id=1, replica_groups=mesh['tok'=8,'voc'=16] {'voc'}, use_global_device_ids=true, to_apply=%region_2.3 | all-reduce | flops 256 | bytes 1792 | tf_op jit(solution)/shard_map/pmax | solution.py:95
  380.4 0.0 copy-done.2
  380.4 3.6 multiply_reduce_fusion
  384.0 35.5 %all-reduce = (f32[128]{0:T(128)S(1)}, f32[128]{0:T(128)S(1)}, f32[128]{0:T(128)S(1)}, f32[128]{0:T(128)S(1)}, f32[128]{0:T(128)S(1)}) all-reduce(f32[128]{0:T(128)S(1)} %get-tuple-element.5, f32[128]{0:T(128)S(1)} %get-tuple-element.4, f32[128]{0:T(128)S(1)} %get-tuple-element.3, ...), channel_id=1, replica_groups=mesh['tok'=8,'voc'=16] {'voc'}, use_global_device_ids=true, to_apply=%region_22.23 | all-reduce | flops 640 | bytes 5120 | tf_op jit(solution)/shard_map/psum | solution.py:97
  419.4 0.5 subtract_subtract_fusion
  420.0 0.0 copy-done.6
  420.0 3.5 multiply_convert_fusion
  423.5 0.0 all-gather.5.cloned.1.call-update
  423.5 0.0 reduce-scatter.8.cloned.1.call-start
  423.6 51.8 %all-gather.5.cloned.1.call-done = bf16[1024,4864]{1,0:T(8,128)(2,1)} async-done(((bf16[128,4864]{1,0:T(8,128)(2,1)}), bf16[1024,4864]{1,0:T(8,128)(2,1)}) %all-gather.5.cloned.1.call-update) | async-done | bytes 9961488 | tf_op jit(solution)/shard_map/all_gather | solution.py:119
  475.4 11.1 %convolution_convert_fusion.3 = bf16[1024,512]{1,0:T(8,128)(2,1)} fusion(bf16[1024,4864]{1,0:T(8,128)(2,1)} %all-gather.5.cloned.1.call-done, bf16[512,4864]{1,0:T(8,128)(2,1)} %param.21), kind=kOutput, calls=%fused_computation.17 | convolution fusion | flops 5100797952 | bytes 15990784 | tf_op jit(solution)/shard_map/dot_general | solution.py:118
  486.5 0.0 reduce-scatter.8.cloned.1.call-update
  486.5 74.6 %reduce-scatter.8.cloned.1.call-done = bf16[64,512]{1,0:T(8,128)(2,1)} async-done(((bf16[1024,512]{1,0:T(8,128)(2,1)}), bf16[64,512]{1,0:T(8,128)(2,1)}) %reduce-scatter.8.cloned.1.call-update) | async-done | bytes 65552 | tf_op jit(solution)/shard_map/reduce_scatter | solution.py:124
  561.1 0.0 copy-done.1
  (9 shorter events, 0.0 us)
Async XLA Ops:
  8.0 59.5 %copy-start = (bf16[384,4096]{1,0:T(8,128)(2,1)S(1)}, bf16[384,4096]{1,0:T(8,128)(2,1)}, u32[]{:S(2)}) copy-start(bf16[384,4096]{1,0:T(8,128)(2,1)} %param.17) | copy-start | bytes 9437188
  78.2 5.0 copy-start.4
  78.2 34.6 %all-to-all-start.1 = ((bf16[128,2,4096]{2,1,0:T(2,128)(2,1)}), bf16[128,2,4096]{2,1,0:T(2,128)(2,1)S(1)}, u32[]{:S(2)}, u32[]{:S(2)}) async-start(bf16[128,2,4096]{2,1,0:T(2,128)(2,1)} %reshape.61), calls=%async_computation.2 | async-start | bytes 4194304 | tf_op jit(solution)/shard_map/all_to_all | solution.py:62
  116.9 2.7 copy-start.3
  116.9 4.0 copy-start.5
  142.6 19.4 %all-to-all-start.3 = ((bf16[128,8,512]{2,0,1:T(8,128)(2,1)}), bf16[128,8,512]{2,0,1:T(8,128)(2,1)S(1)}, u32[]{:S(2)}, u32[]{:S(2)}) async-start(bf16[128,8,512]{2,0,1:T(8,128)(2,1)} %copy.16), calls=%async_computation.4 | async-start | bytes 2097152 | tf_op jit(solution)/shard_map/all_to_all | solution.py:71
  146.2 44.2 %all-gather.3.cloned.1.call-start = ((), (), s32[]{:S(2)}) async-start(), calls=%async_computation.7 | async-start | bytes 1114112 | tf_op jit(solution)/shard_map/all_gather | solution.py:72
  146.9 81.6 %reduce-scatter.6.cloned.1.call-start = ((), (), s32[]{:S(2)}) async-start(), calls=%async_computation.9 | async-start | bytes 11206656 | tf_op jit(solution)/shard_map/reduce_scatter | solution.py:75
  172.3 164.8 %reduce-scatter.4.cloned.1.call-start = ((), (), s32[]{:S(2)}) async-start(), calls=%async_computation.8 | async-start | bytes 22413312 | tf_op jit(solution)/shard_map/reduce_scatter | solution.py:82
  202.8 0.7 copy-start.7
  202.8 272.5 %all-gather.5.cloned.1.call-start = ((), (), s32[]{:S(2)}) async-start(), calls=%async_computation.10 | async-start | bytes 11206656 | tf_op jit(solution)/shard_map/all_gather | solution.py:119
  337.0 43.4 %copy-start.2 = (f32[128,4864]{1,0:T(8,128)S(1)}, f32[128,4864]{1,0:T(8,128)}, u32[]{:S(2)}) copy-start(f32[128,4864]{1,0:T(8,128)} %reduce-scatter.4.cloned.1.call-done) | copy-start | bytes 7471108
  339.1 80.9 %copy-start.6 = (f32[128]{0:T(128)S(1)}, f32[128]{0:T(128)}, u32[]{:S(2)}) copy-start(f32[128]{0:T(128)} %param.23) | copy-start | bytes 1540
  423.5 137.6 %reduce-scatter.8.cloned.1.call-start = ((), (), s32[]{:S(2)}) async-start(), calls=%async_computation.11 | async-start | bytes 1114112 | tf_op jit(solution)/shard_map/reduce_scatter | solution.py:124
  475.4 85.7 %copy-start.1 = (bf16[384,4096]{1,0:T(8,128)(2,1)S(1)}, bf16[384,4096]{1,0:T(8,128)(2,1)}, u32[]{:S(2)}) copy-start(bf16[384,4096]{1,0:T(8,128)(2,1)} %param.17) | copy-start | bytes 9437188
Sparse Core Ops, SparseCore 0:
  149.1 41.1 all-gather.2
  486.6 74.4 reduce-scatter.7
Sparse Core Ops, SparseCore 1:
  172.3 56.1 reduce-scatter.5
  230.9 106.1 reduce-scatter.3
  423.6 51.7 all-gather.4
